TPU v7x, 256 devices: a whole 4x4x8 slice. The times are simulated.
256 devices in a mesh: blk: 16 (over y, z_lo, core), dp: 16 (over z_hi, x).
Axes of the slice: x: 4, y: 4, z: 8 (z_hi: 4, z_lo: 2; z = z_hi * 2 + z_lo), core: 2. Of those that a mesh axis runs over, the one named last changes fastest.
Arguments:
- queries: bfloat16 [32768, 256], P(('blk', 'dp')), may hold values from -30 to 30, as said below
- pois: bfloat16 [32768, 256], P(('blk', 'dp')), may hold values from -4 to 4, as said below
- query_region: int32 [32768], P(('blk', 'dp')), may hold values from 0 to 63
- block_region: int32 [256], P(('blk', 'dp')), may hold values from 0 to 63
- region_mask: int32 [64, 64], replicated, may hold values from 0 to 1
- positive: int32 [32768], P(('blk', 'dp')), may hold values from 0 to 32767
Outputs:
- loss: float32 [32768], P(('blk', 'dp'))
- query_grad: float32 [32768, 256], P(('blk', 'dp'))
- poi_grad: float32 [32768, 256], P(('blk', 'dp'))
Inputs may be any that keep to these rules, and one draw needn't show every extreme that they name: `queries`: float entries. `pois`: float entries.
All inputs are finite; a program needn't handle non-finite values.
Results may differ from a plain program's by a relative error of at most 0.00185.
Values may be sent and summed in bfloat16 or wider, within the bound.
A program may use at most 64 MiB of HBM per device.

v0:
```python
import math
import jax
import jax.numpy as jnp
from jax import lax
from jax.sharding import PartitionSpec as P

TILE = 128
floor_value = -1e30


def shifted(x, axis, by):
    length = lax.axis_size(axis)
    return lax.ppermute(x, axis, [(i, (i + by) % length) for i in range(length)])


def combined_all(x, axis, combine):
    everything = jax.tree.map(lambda part: lax.all_gather(part, axis), x)
    leading = jax.tree.map(lambda part: part[0], everything)

    def lap(k, so_far):
        return combine(so_far, jax.tree.map(lambda part: part[k], everything))

    return lax.fori_loop(1, lax.axis_size(axis), lap, leading)


def combine_parts(first, second):
    highest = jnp.maximum(first[0], second[0])
    total = first[1] * jnp.exp(first[0] - highest) + second[1] * jnp.exp(second[0] - highest)
    return (highest, total, first[2] + second[2])


def body(queries, pois, query_region, block_region, region_mask, positive):
    group_count = lax.axis_size("dp")
    cycle_count = lax.axis_size("blk")
    cycle_index = lax.axis_index("blk")
    group_index = lax.axis_index("dp")
    slab_rows = pois.shape[0]
    own_rows = queries.shape[0]
    width = queries.shape[1]
    regions = region_mask.shape[0]
    scale = 1.0 / math.sqrt(width)
    group_q = lax.all_gather(queries, "dp", axis=0, tiled=True)
    group_reg, group_pos = (
        lax.all_gather(query_region, "dp", axis=0, tiled=True),
        lax.all_gather(positive, "dp", axis=0, tiled=True),
    )
    block_all = lax.all_gather(block_region, ("blk", "dp"), axis=0, tiled=True)
    group_rows = group_q.shape[0]
    region_ids = jnp.arange(regions, dtype=jnp.int32)
    query_hot = (group_reg[:, None] == region_ids[None, :]).astype(jnp.bfloat16)
    block_hot = (block_all[:, None] == region_ids[None, :]).astype(jnp.bfloat16)
    mask_rows = jnp.dot(
        query_hot, region_mask.astype(jnp.bfloat16), preferred_element_type=jnp.float32
    ).astype(jnp.bfloat16)
    block_open = (
        lax.dot_general(
            mask_rows, block_hot, (((1,), (1,)), ((), ())), preferred_element_type=jnp.float32
        )
        > 0.5
    )
    pos_block = group_pos // TILE

    def anchor_start(anchor):
        return (anchor % cycle_count * group_count + group_index) * slab_rows

    def piece_masks(start, count):
        columns = start + jnp.arange(count, dtype=jnp.int32)
        blocks = columns // TILE
        opened = jnp.take(block_open, blocks, axis=1) | (blocks[None, :] == pos_block[:, None])
        is_pos = columns[None, :] == group_pos[:, None]
        return (opened, is_pos)

    def logits(slab):
        return (
            lax.dot_general(
                group_q, slab, (((1,), (1,)), ((), ())), preferred_element_type=jnp.float32
            )
            * scale
        )

    def forward_piece(state, slab, start):
        opened, is_pos = piece_masks(start, slab.shape[0])
        highest, total, pos_score = state
        scores = logits(slab)
        masked = jnp.where(opened, scores, floor_value)
        new_high = jnp.maximum(highest, jnp.max(masked, axis=1))
        total = total * jnp.exp(highest - new_high) + jnp.sum(
            jnp.where(opened, jnp.exp(scores - new_high[:, None]), 0.0), axis=1
        )
        pos_score = pos_score + jnp.sum(jnp.where(is_pos, scores, 0.0), axis=1)
        return (new_high, total, pos_score)

    def backward_piece(query_acc, slab, start, log_total):
        opened, is_pos = piece_masks(start, slab.shape[0])
        current = query_acc
        scores = logits(slab)
        weights = (
            jnp.where(opened, jnp.exp(scores - log_total[:, None]), 0.0)
            - is_pos.astype(jnp.float32)
        ).astype(jnp.bfloat16)
        current = current + jnp.dot(weights, slab, preferred_element_type=jnp.float32)
        tile_grad = lax.dot_general(
            weights, group_q, (((0,), (0,)), ((), ())), preferred_element_type=jnp.float32
        )
        return (current, tile_grad)

    initial = (
        jnp.full((group_rows,), floor_value, jnp.float32),
        jnp.zeros((group_rows,), jnp.float32),
        jnp.zeros((group_rows,), jnp.float32),
    )
    query_acc = jnp.zeros((group_rows, width), jnp.float32)
    state = forward_piece(initial, pois, anchor_start(cycle_index))

    def forward_step(step, carry):
        slab, current = carry
        slab = shifted(slab, "blk", 1)
        return (slab, forward_piece(current, slab, anchor_start(cycle_index - step)))

    unused, state = lax.fori_loop(1, cycle_count, forward_step, (pois, state))
    highest, total, pos_score = combined_all(state, "dp", combine_parts)
    log_total = highest + jnp.log(total)
    losses = log_total - pos_score
    loss = lax.dynamic_slice_in_dim(losses, group_index * own_rows, own_rows, 0)

    def backward_step(step, carry):
        slab, grads, current = carry
        current, tile_grad = backward_piece(
            current, slab, anchor_start(cycle_index - step), log_total
        )
        grads = grads + tile_grad
        slab = shifted(slab, "blk", 1)
        grads = shifted(grads, "blk", 1)
        return (slab, grads, current)

    start_grads = jnp.zeros((slab_rows, width), jnp.float32)
    unused, poi_sum, query_acc = lax.fori_loop(
        0, cycle_count, backward_step, (pois, start_grads, query_acc)
    )
    query_grad = lax.psum_scatter(query_acc * scale, "dp", scatter_dimension=0, tiled=True)
    return (loss, query_grad, poi_sum * scale)


def solution(mesh):
    in_specs = (
        P(("blk", "dp"), None),
        P(("blk", "dp"), None),
        P(("blk", "dp")),
        P(("blk", "dp")),
        P(),
        P(("blk", "dp")),
    )
    out_specs = (P(("blk", "dp")), P(("blk", "dp"), None), P(("blk", "dp"), None))
    return jax.shard_map(body, mesh=mesh, in_specs=in_specs, out_specs=out_specs, check_vma=False)
```

profile of v0, /device:TPU:8, one launch (start us, length us, event | category | flops | bytes accessed | tf_op | source)
XLA Modules:
  0.0 693.0 jit_solution(1324821323674346143)
XLA Ops:
  8.9 80.1 %all-reduce = s32[256]{0:T(256)S(1)} all-reduce(s32[256]{0:T(256)S(1)} %dynamic-update-slice), channel_id=1, replica_groups=mesh['blk'=16,'dp'=16] {'blk','dp'}, use_global_device_ids=true, to_apply=%add | all-reduce | flops 256 | bytes 2048
  89.1 41.1 %all-gather.3 = s32[16,1,128]{2,1,0:T(1,128)S(1)} all-gather(s32[1,1,128]{2,1,0:T(1,128)} %bitcast.66), channel_id=1, replica_groups=mesh['blk'=16,'dp'=16] {'dp'}, dimensions={0}, use_global_device_ids=true | all-gather | bytes 8704 | tf_op jit(solution)/shard_map/all_gather | solution.py:44
  134.5 37.8 %all-gather.4 = s32[16,1,128]{2,1,0:T(1,128)S(1)} all-gather(s32[1,1,128]{2,1,0:T(1,128)S(1)} %bitcast.67), channel_id=1, replica_groups=mesh['blk'=16,'dp'=16] {'dp'}, dimensions={0}, use_global_device_ids=true | all-gather | bytes 8704 | tf_op jit(solution)/shard_map/all_gather | solution.py:45
  174.7 110.5 %while.60 = (s32[]{:T(128)}, bf16[128,256]{1,0:T(8,128)(2,1)S(1)}, f32[2048]{0:T(1024)S(1)}, f32[2048]{0:T(1024)S(1)}, f32[2048]{0:T(1024)S(1)}, /*index=5*/s32[...) while((s32[]{:T(128)}, bf16[128,256]{1,0:T(8,128)(2,1)S(1)}, ...), condition=%wide.region_7.9_spmd, body=%wide.region_3.8_spmd.sunk | while | flops 138162320 | bytes 4825830 | solution.py:120
  176.5 2.8 collective-permute-done
  183.6 2.8 collective-permute-done
  190.8 2.8 collective-permute-done
  254.7 3.0 collective-permute-done
  262.0 4.1 collective-permute-done
  270.4 4.1 collective-permute-done
  278.7 4.1 collective-permute-done
  285.2 39.0 %all-gather = f32[32768]{0:T(1024)S(1)} all-gather(f32[2048]{0:T(1024)S(1)} %get-tuple-element.719), channel_id=2, replica_groups=mesh['blk'=16,'dp'=16] {'dp'}, dimensions={0}, use_global_device_ids=true | all-gather | bytes 139264 | tf_op jit(solution)/shard_map/all_gather | solution.py:17
  324.2 40.4 %all-gather.1 = f32[32768]{0:T(1024)S(1)} all-gather(f32[2048]{0:T(1024)S(1)} %get-tuple-element.720), channel_id=3, replica_groups=mesh['blk'=16,'dp'=16] {'dp'}, dimensions={0}, use_global_device_ids=true | all-gather | bytes 139264 | tf_op jit(solution)/shard_map/all_gather | solution.py:17
  364.6 39.2 %all-gather.2 = f32[32768]{0:T(1024)S(1)} all-gather(f32[2048]{0:T(1024)S(1)} %get-tuple-element.721), channel_id=4, replica_groups=mesh['blk'=16,'dp'=16] {'dp'}, dimensions={0}, use_global_device_ids=true | all-gather | bytes 139264 | tf_op jit(solution)/shard_map/all_gather | solution.py:17
  406.0 178.6 %while.62 = (s32[]{:T(128)}, bf16[128,256]{1,0:T(8,128)(2,1)S(1)}, f32[128,256]{1,0:T(8,128)S(1)}, f32[2048,256]{1,0:T(8,128)S(1)}, s32[]{:T(128)}, /*index=5*/s...) while((s32[]{:T(128)}, bf16[128,256]{1,0:T(8,128)(2,1)S(1)}, ...), condition=%wide.region_11.13_spmd.clone, body=%wide.region_10.12_spmd.clone.sunk | while | flops 406362368 | bytes 14713012 | solution.py:137
  411.6 4.6 collective-permute-done.2
  422.7 5.4 collective-permute-done.2
  433.6 4.6 collective-permute-done.2
  444.6 5.4 collective-permute-done.2
  455.8 5.4 collective-permute-done.2
  467.0 5.4 collective-permute-done.2
  478.3 5.4 collective-permute-done.2
  489.5 5.4 collective-permute-done.2
  500.7 5.4 collective-permute-done.2
  511.9 5.4 collective-permute-done.2
  523.1 5.4 collective-permute-done.2
  534.4 5.4 collective-permute-done.2
  545.6 5.4 collective-permute-done.2
  556.8 5.4 collective-permute-done.2
  568.0 5.4 collective-permute-done.2
  579.2 5.4 collective-permute-done.2
  588.1 98.1 %reduce-scatter.2.cloned.1.call-done = f32[128,256]{1,0:T(8,128)} async-done(((f32[2048,256]{1,0:T(8,128)}), f32[128,256]{1,0:T(8,128)}) %reduce-scatter.2.cloned.1.call-update) | async-done | bytes 131088 | tf_op jit(solution)/shard_map/reduce_scatter | solution.py:140
  (541 shorter events, 190.7 us)
Async XLA Ops:
  7.2 165.1 %all-gather.7.cloned.1.call-start = ((), (), s32[]{:S(2)}) async-start(), calls=%async_computation.1 | async-start | bytes 1114112 | tf_op jit(solution)/shard_map/all_gather | solution.py:42
  8.1 678.1 %reduce-scatter.2.cloned.1.call-start = ((), (), s32[]{:S(2)}) async-start(), calls=%async_computation.2 | async-start | bytes 2228224 | tf_op jit(solution)/shard_map/reduce_scatter | solution.py:140
  260.2 5.9 collective-permute-start
  268.5 5.9 collective-permute-start
  276.9 5.9 collective-permute-start
  416.2 6.6 collective-permute-start.1
  420.8 7.3 %collective-permute-start.2 = (f32[128,256]{1,0:T(8,128)S(1)}, f32[128,256]{1,0:T(8,128)S(1)}, u32[]{:S(2)}, u32[]{:S(2)}) collective-permute-start(f32[128,256]{1,0:T(8,128)S(1)} %convolution_add_fusion.4), channel_id=1, source_target_pairs={{0,16},{16,32},{32,48},{48,64},{64,80},{80,96},{96,112},{112,128},... | collective-permute-start | bytes 393224 | tf_op jit(solution)/shard_map/while/body/eval_jaxpr/ppermute | solution.py:13
  438.2 6.5 collective-permute-start.1
  442.8 7.2 %collective-permute-start.2 = (f32[128,256]{1,0:T(8,128)S(1)}, f32[128,256]{1,0:T(8,128)S(1)}, u32[]{:S(2)}, u32[]{:S(2)}) collective-permute-start(f32[128,256]{1,0:T(8,128)S(1)} %convolution_add_fusion.4), channel_id=1, source_target_pairs={{0,16},{16,32},{32,48},{48,64},{64,80},{80,96},{96,112},{112,128},... | collective-permute-start | bytes 393224 | tf_op jit(solution)/shard_map/while/body/eval_jaxpr/ppermute | solution.py:13
  454.7 6.6 collective-permute-start.2
  461.2 5.8 collective-permute-start.1
  465.9 6.6 collective-permute-start.2
  472.5 5.8 collective-permute-start.1
  477.1 6.6 collective-permute-start.2
  483.7 5.8 collective-permute-start.1
  488.3 6.6 collective-permute-start.2
  494.9 5.8 collective-permute-start.1
  499.5 6.6 collective-permute-start.2
  506.1 5.8 collective-permute-start.1
  510.7 6.6 collective-permute-start.2
  517.3 5.8 collective-permute-start.1
  522.0 6.6 collective-permute-start.2
  528.5 5.8 collective-permute-start.1
  533.2 6.6 collective-permute-start.2
  539.8 5.8 collective-permute-start.1
  544.4 6.6 collective-permute-start.2
  551.0 5.8 collective-permute-start.1
  555.6 6.6 collective-permute-start.2
  562.2 5.8 collective-permute-start.1
  566.8 6.6 collective-permute-start.2
  573.4 5.8 collective-permute-start.1
  578.0 6.6 collective-permute-start.2
  (35 other events, 122.0 us)
Sparse Core Ops, SparseCore 0:
  10.4 56.3 all-gather.6
  586.3 99.8 reduce-scatter.1
where the time goes:
time: 694 us; the launch traced here: 693 us
  blocking collectives  278 us (40%)
  waiting for transfers between devices  236 us (34%)
  matrix products  81.3 us (12%)
  local copies, waits for them, and re-layouts  60.6 us (9%)
  other arithmetic  15.1 us (2%)
  between operations  14.9 us (2%)
    ppermute x47, waiting for transfers between devices, shifted(): lax.ppermute(x, axis, [(i, (i + by) % length) for i in range(length)])  138 us
    all_gather x3, blocking collectives, combined_all(): everything = jax.tree.map(lambda part: lax.all_gather(part, axis), x)  119 us
    reduce_scatter x1, waiting for transfers between devices, body(): lax.psum_scatter(query_acc * scale, 'dp', scatter_dimension=0, tiled=True)  98.1 us
    unnamed x1, blocking collectives  80.1 us
    dot_general x32, matrix products, logits(): lax.dot_general(group_q, slab, (((1,), (1,)), ((), ())), preferred_elemen...  63 us
    gather x48, local copies, waits for them, and re-layouts, piece_masks(): jnp.take(block_open, blocks, axis=1)  57.7 us
    all_gather x1, blocking collectives, body(): lax.all_gather(query_region, 'dp', axis=0, tiled=True)  41.1 us
    all_gather x1, blocking collectives, body(): lax.all_gather(positive, 'dp', axis=0, tiled=True)  37.8 us
  transfers between devices with their start and end apart: 49, of which 46 were waited for; matrix products, arithmetic and copies ran while one was open for 17% of the time, Pallas kernels for 0%

commit v1 on v0

--- a/solution.py
+++ b/solution.py
@@ -42,7 +42,9 @@
     group_q = lax.all_gather(queries, "dp", axis=0, tiled=True)
     group_reg, group_pos = (
         lax.all_gather(query_region, "dp", axis=0, tiled=True),
-        lax.all_gather(positive, "dp", axis=0, tiled=True),
+        jnp.concatenate(
+            lax.all_to_all(jnp.stack([positive] * lax.axis_size("dp")), "dp", 0, 0), axis=0
+        ),
     )
     block_all = lax.all_gather(block_region, ("blk", "dp"), axis=0, tiled=True)
     group_rows = group_q.shape[0]

time: 694 us -> 665 us (0.958)
  blocking collectives: 278 us -> 237 us
  starting transfers between devices: 2.78 us -> 13.8 us
    all_gather x1 -> x0, blocking collectives: 37.8 us -> none  [body(): lax.all_gather(positive, 'dp', axis=0, tiled=True)]
    all_to_all x0 -> x1, starting transfers between devices: none -> 11 us  [body(): lax.all_to_all(jnp.stack([positive] * lax.axis_size('dp')), 'dp', 0, 0)]
  transfers between devices with their start and end apart: 49 -> 50, of which waited for: 46 -> 46; matrix products, arithmetic and copies ran while one was open for 17% -> 18% of each run, Pallas kernels for 0% -> 0%
where the time goes in v1:
time: 665 us; the launch traced here: 664 us
  blocking collectives  237 us (36%)
  waiting for transfers between devices  235 us (35%)
  matrix products  81.3 us (12%)
  local copies, waits for them, and re-layouts  61.9 us (9%)
  other arithmetic  15.1 us (2%)
  between operations  14.9 us (2%)
  starting transfers between devices  13.8 us (2%)
    ppermute x47, waiting for transfers between devices, shifted(): lax.ppermute(x, axis, [(i, (i + by) % length) for i in range(length)])  137 us
    all_gather x3, blocking collectives, combined_all(): everything = jax.tree.map(lambda part: lax.all_gather(part, axis), x)  119 us
    reduce_scatter x1, waiting for transfers between devices, body(): lax.psum_scatter(query_acc * scale, 'dp', scatter_dimension=0, tiled=True)  98.2 us
    unnamed x1, blocking collectives  77.3 us
    dot_general x32, matrix products, logits(): lax.dot_general(group_q, slab, (((1,), (1,)), ((), ())), preferred_elemen...  63 us
    gather x48, local copies, waits for them, and re-layouts, piece_masks(): jnp.take(block_open, blocks, axis=1)  57.7 us
    all_gather x1, blocking collectives, body(): lax.all_gather(query_region, 'dp', axis=0, tiled=True)  40.6 us
  transfers between devices with their start and end apart: 50, of which 46 were waited for; matrix products, arithmetic and copies ran while one was open for 18% of the time, Pallas kernels for 0%

profile of v1, /device:TPU:8, one launch (start us, length us, event | category | flops | bytes accessed | tf_op | source)
XLA Modules:
  0.0 663.5 jit_solution(8499687813709630585)
XLA Ops:
  9.3 11.0 %all-to-all-start = ((s32[16,1,128]{2,1,0:T(1,128)}), s32[16,1,128]{2,1,0:T(1,128)S(1)}, u32[]{:S(2)}, u32[]{:S(2)}) async-start(s32[16,1,128]{2,1,0:T(1,128)} %stack.2), calls=%async_computation | async-start | bytes 16384 | tf_op jit(solution)/shard_map/all_to_all | solution.py:46
  21.2 77.3 %all-reduce = s32[256]{0:T(256)S(1)} all-reduce(s32[256]{0:T(256)S(1)} %dynamic-update-slice), channel_id=1, replica_groups=mesh['blk'=16,'dp'=16] {'blk','dp'}, use_global_device_ids=true, to_apply=%add | all-reduce | flops 256 | bytes 2048
  98.5 40.6 %all-gather.3 = s32[16,1,128]{2,1,0:T(1,128)S(1)} all-gather(s32[1,1,128]{2,1,0:T(1,128)} %bitcast.74), channel_id=1, replica_groups=mesh['blk'=16,'dp'=16] {'dp'}, dimensions={0}, use_global_device_ids=true | all-gather | bytes 8704 | tf_op jit(solution)/shard_map/all_gather | solution.py:44
  145.9 109.5 %while.60 = (s32[]{:T(128)}, bf16[128,256]{1,0:T(8,128)(2,1)S(1)}, f32[2048]{0:T(1024)S(1)}, f32[2048]{0:T(1024)S(1)}, f32[2048]{0:T(1024)S(1)}, /*index=5*/s32[...) while((s32[]{:T(128)}, bf16[128,256]{1,0:T(8,128)(2,1)S(1)}, ...), condition=%wide.region_7.9_spmd, body=%wide.region_3.8_spmd.sunk | while | flops 138162320 | bytes 4825830 | solution.py:122
  147.7 2.8 collective-permute-done
  154.8 2.8 collective-permute-done
  161.9 2.8 collective-permute-done
  169.0 2.8 collective-permute-done
  233.0 3.3 collective-permute-done
  240.6 4.1 collective-permute-done
  248.9 4.1 collective-permute-done
  255.4 39.4 %all-gather = f32[32768]{0:T(1024)S(1)} all-gather(f32[2048]{0:T(1024)S(1)} %get-tuple-element.719), channel_id=2, replica_groups=mesh['blk'=16,'dp'=16] {'dp'}, dimensions={0}, use_global_device_ids=true | all-gather | bytes 139264 | tf_op jit(solution)/shard_map/all_gather | solution.py:17
  294.9 40.0 %all-gather.1 = f32[32768]{0:T(1024)S(1)} all-gather(f32[2048]{0:T(1024)S(1)} %get-tuple-element.720), channel_id=3, replica_groups=mesh['blk'=16,'dp'=16] {'dp'}, dimensions={0}, use_global_device_ids=true | all-gather | bytes 139264 | tf_op jit(solution)/shard_map/all_gather | solution.py:17
  334.9 39.5 %all-gather.2 = f32[32768]{0:T(1024)S(1)} all-gather(f32[2048]{0:T(1024)S(1)} %get-tuple-element.721), channel_id=4, replica_groups=mesh['blk'=16,'dp'=16] {'dp'}, dimensions={0}, use_global_device_ids=true | all-gather | bytes 139264 | tf_op jit(solution)/shard_map/all_gather | solution.py:17
  376.7 178.4 %while.62 = (s32[]{:T(128)}, bf16[128,256]{1,0:T(8,128)(2,1)S(1)}, f32[128,256]{1,0:T(8,128)S(1)}, f32[2048,256]{1,0:T(8,128)S(1)}, s32[]{:T(128)}, /*index=5*/s...) while((s32[]{:T(128)}, bf16[128,256]{1,0:T(8,128)(2,1)S(1)}, ...), condition=%wide.region_11.13_spmd.clone, body=%wide.region_10.12_spmd.clone.sunk | while | flops 406362368 | bytes 14713012 | solution.py:139
  382.2 4.6 collective-permute-done.2
  393.3 5.4 collective-permute-done.2
  404.2 4.5 collective-permute-done.2
  415.0 5.4 collective-permute-done.2
  426.3 5.4 collective-permute-done.2
  437.5 5.4 collective-permute-done.2
  448.7 5.4 collective-permute-done.2
  459.9 5.4 collective-permute-done.2
  471.1 5.4 collective-permute-done.2
  482.4 5.4 collective-permute-done.2
  493.6 5.4 collective-permute-done.2
  504.8 5.4 collective-permute-done.2
  516.0 5.4 collective-permute-done.2
  527.2 5.4 collective-permute-done.2
  538.4 5.4 collective-permute-done.2
  549.7 5.4 collective-permute-done.2
  558.5 98.2 %reduce-scatter.2.cloned.1.call-done = f32[128,256]{1,0:T(8,128)} async-done(((f32[2048,256]{1,0:T(8,128)}), f32[128,256]{1,0:T(8,128)}) %reduce-scatter.2.cloned.1.call-update) | async-done | bytes 131088 | tf_op jit(solution)/shard_map/reduce_scatter | solution.py:142
  (541 shorter events, 191.8 us)
Async XLA Ops:
  7.2 136.3 %all-gather.6.cloned.1.call-start = ((), (), s32[]{:S(2)}) async-start(), calls=%async_computation.2 | async-start | bytes 1114112 | tf_op jit(solution)/shard_map/all_gather | solution.py:42
  9.3 134.1 %all-to-all-start = ((s32[16,1,128]{2,1,0:T(1,128)}), s32[16,1,128]{2,1,0:T(1,128)S(1)}, u32[]{:S(2)}, u32[]{:S(2)}) async-start(s32[16,1,128]{2,1,0:T(1,128)} %stack.2), calls=%async_computation | async-start | bytes 16384 | tf_op jit(solution)/shard_map/all_to_all | solution.py:46
  20.4 636.3 %reduce-scatter.2.cloned.1.call-start = ((), (), s32[]{:S(2)}) async-start(), calls=%async_computation.3 | async-start | bytes 2228224 | tf_op jit(solution)/shard_map/reduce_scatter | solution.py:142
  238.8 5.9 collective-permute-start
  247.1 5.9 collective-permute-start
  386.8 6.5 collective-permute-start.1
  391.4 7.3 %collective-permute-start.2 = (f32[128,256]{1,0:T(8,128)S(1)}, f32[128,256]{1,0:T(8,128)S(1)}, u32[]{:S(2)}, u32[]{:S(2)}) collective-permute-start(f32[128,256]{1,0:T(8,128)S(1)} %convolution_add_fusion.4), channel_id=1, source_target_pairs={{0,16},{16,32},{32,48},{48,64},{64,80},{80,96},{96,112},{112,128},... | collective-permute-start | bytes 393224 | tf_op jit(solution)/shard_map/while/body/eval_jaxpr/ppermute | solution.py:13
  408.7 6.3 collective-permute-start.1
  413.3 7.1 %collective-permute-start.2 = (f32[128,256]{1,0:T(8,128)S(1)}, f32[128,256]{1,0:T(8,128)S(1)}, u32[]{:S(2)}, u32[]{:S(2)}) collective-permute-start(f32[128,256]{1,0:T(8,128)S(1)} %convolution_add_fusion.4), channel_id=1, source_target_pairs={{0,16},{16,32},{32,48},{48,64},{64,80},{80,96},{96,112},{112,128},... | collective-permute-start | bytes 393224 | tf_op jit(solution)/shard_map/while/body/eval_jaxpr/ppermute | solution.py:13
  420.5 5.8 collective-permute-start.1
  425.1 6.6 collective-permute-start.2
  436.3 6.6 collective-permute-start.2
  442.9 5.8 collective-permute-start.1
  447.5 6.6 collective-permute-start.2
  454.1 5.8 collective-permute-start.1
  458.7 6.6 collective-permute-start.2
  465.3 5.8 collective-permute-start.1
  470.0 6.6 collective-permute-start.2
  476.6 5.8 collective-permute-start.1
  481.2 6.6 collective-permute-start.2
  487.8 5.8 collective-permute-start.1
  492.4 6.6 collective-permute-start.2
  499.0 5.8 collective-permute-start.1
  503.6 6.6 collective-permute-start.2
  510.2 5.8 collective-permute-start.1
  514.8 6.6 collective-permute-start.2
  521.4 5.8 collective-permute-start.1
  526.0 6.6 collective-permute-start.2
  532.6 5.8 collective-permute-start.1
  537.3 6.6 collective-permute-start.2
  543.9 5.8 collective-permute-start.1
  548.5 6.6 collective-permute-start.2
  (35 other events, 124.2 us)
Sparse Core Ops, SparseCore 0:
  10.4 55.9 all-gather.5
  556.7 99.9 reduce-scatter.1
